TPU v7x, 256 devices: a whole 4x4x8 slice. The times are simulated.
256 devices in a mesh: seq: 64 (over z, y, x_hi), mdl: 4 (over x_lo, core).
Axes of the slice: x: 4 (x_hi: 2, x_lo: 2; x = x_hi * 2 + x_lo), y: 4, z: 8, core: 2. Of those that a mesh axis runs over, the one named last changes fastest.
Arguments:
- tokens: bfloat16 [16384, 2048], P('seq', 'mdl'), may hold values from -6 to 6
- norm_gain: bfloat16 [2048], P('mdl'), may hold values from 0.099609375 to 1.8984375
- w_query: bfloat16 [2048, 2048], P('seq', 'mdl'), may hold values from -0.125 to 0.125
- key_matrix: bfloat16 [2048, 1024], P('seq', 'mdl'), may hold values from -0.125 to 0.125
- value_matrix: bfloat16 [2048, 1024], P('seq', 'mdl'), may hold values from -0.125 to 0.125
- w_gate: bfloat16 [2048, 2048], P('seq', 'mdl'), may hold values from -0.125 to 0.125
- q_gain: float32 [128], replicated, may hold values from 0.6 to 8
- k_gain: float32 [128], replicated, may hold values from 0.6 to 8
- w_out: bfloat16 [2048, 2048], P('mdl', 'seq'), may hold values from -0.125 to 0.125
- prompt_lengths: int32 [64], replicated, may hold values from 1 to 512, as said below
- segment_ids: int32 [16384], P('seq'), may hold values from 0 to 63, as said below
- tenant_ranges: int32 [4, 2], replicated, may hold values from 0 to 64, as said below
- key_mask: int32 [16384], P('seq'), may hold values 0 or 1
- cache_slot: int32 [64], replicated, may hold values from 0 to 63, each once
Outputs:
- layer_out: bfloat16 [16384, 2048], P('seq', 'mdl')
- cache_keys: bfloat16 [64, 512, 1024], P('seq', None, 'mdl')
- cache_values: bfloat16 [64, 512, 1024], P('seq', None, 'mdl')
Inputs may be any that keep to these rules, and one draw needn't show every extreme that they name: `prompt_lengths`: the lengths sum to 16384 and one of them equals 512. `segment_ids`: request r holds the prompt_lengths[r] consecutive tokens that follow those of requests 0 to r - 1. `tenant_ranges`: each row (lo, hi) has lo < hi; the rows increase and do not intersect; the first lo is 0 and the last hi is 64; request lo of a tenant is its shared prompt. `cache_slot`: each slot belongs to one request.
All inputs are finite; a program needn't handle non-finite values. No bound on the sum of `key_mask` on one device may be relied on, other than what follows from the above.
Results may differ from a plain program's by a relative error of at most 0.012.
The roundings to bfloat16 on the way count: a program that leaves them out, or rounds other values in their place, can miss the bound.
Values may be sent and summed in bfloat16 or wider, within the bound.
A program may use at most 128 MiB of HBM per device.

v0:
```python
import math
import jax
import jax.numpy as jnp
from jax import lax
from jax.sharding import PartitionSpec as P

HEAD_SIZE = 128
LMAX = 512
epsilon = 1e-06
rope_base = 1000000.0
masked_score = -1e30


def head_norm(values, gain_vector):
    return (
        values
        * lax.rsqrt(jnp.mean(values * values, axis=-1, keepdims=True) + epsilon)
        * gain_vector
    )


def rotate(values, position):
    half_width = values.shape[-1] // 2
    frequency = rope_base ** (-2.0 * jnp.arange(half_width, dtype=jnp.float32) / values.shape[-1])
    angles = position.astype(jnp.float32)[:, None] * frequency[None, :]
    cosine = jnp.cos(angles)[:, None, :]
    sine_part = jnp.sin(angles)[:, None, :]
    former = values[..., :half_width]
    latter = values[..., half_width:]
    return jnp.concatenate(
        [former * cosine - latter * sine_part, latter * cosine + former * sine_part], axis=-1
    )


def token_tables(lengths, segments, ranges):
    request_count = lengths.shape[0]
    starts = jnp.cumsum(lengths) - lengths
    requests = jnp.arange(request_count, dtype=jnp.int32)
    member = (requests[:, None] > ranges[None, :, 0]) & (requests[:, None] < ranges[None, :, 1])
    shared_of = jnp.sum(jnp.where(member, ranges[None, :, 0] + 3, 0), axis=1) - 3
    onehot = segments[:, None] == requests[None, :]
    seg_start = jnp.sum(jnp.where(onehot, starts[None, :], 0), axis=1)
    shared_req = jnp.sum(jnp.where(onehot, shared_of[None, :], 0), axis=1)
    return (starts, seg_start, shared_req)


def body(
    tokens,
    norm_gain,
    w_query,
    key_matrix,
    value_matrix,
    w_gate,
    q_gain,
    k_gain,
    w_out,
    prompt_lengths,
    segment_ids,
    tenant_ranges,
    key_mask,
    cache_slot,
):
    local_rows = tokens.shape[0]
    wide_tokens = tokens.astype(jnp.float32)
    full_width = tokens.shape[1] * lax.axis_size("mdl")
    square_total = lax.psum(jnp.sum(wide_tokens * wide_tokens, axis=1), "mdl")
    scaled = (
        wide_tokens
        * lax.rsqrt(square_total / full_width + epsilon)[:, None]
        * norm_gain.astype(jnp.float32)
    )
    normalized_input = lax.all_gather(scaled.astype(jnp.bfloat16), "mdl", axis=1, tiled=True)
    pieces = (
        lax.all_gather(w_query, "seq", axis=0, tiled=True),
        lax.all_gather(key_matrix, "seq", axis=0, tiled=True),
        lax.all_gather(value_matrix, "seq", axis=0, tiled=True),
        lax.all_gather(w_gate, "seq", axis=0, tiled=True),
    )
    columns = normalized_input
    query_rows, unprojected_keys, values_raw, gate_logits = tuple(
        (
            jnp.dot(columns, weight_part, preferred_element_type=jnp.float32)
            for weight_part in pieces
        )
    )
    device_seq = lax.axis_index("seq")
    token_ids = device_seq * local_rows + jnp.arange(local_rows, dtype=jnp.int32)
    starts, seg_start, shared_req = token_tables(prompt_lengths, segment_ids, tenant_ranges)
    position = token_ids - seg_start
    query_heads = query_rows.shape[1] // HEAD_SIZE
    kv_heads = unprojected_keys.shape[1] // HEAD_SIZE
    query_group_width = query_heads // kv_heads
    query_rows = (
        rotate(head_norm(query_rows.reshape(local_rows, query_heads, HEAD_SIZE), q_gain), position)
        .astype(jnp.bfloat16)
        .reshape(local_rows, kv_heads, query_group_width, HEAD_SIZE)
    )
    flat_keys = (
        rotate(
            head_norm(unprojected_keys.reshape(local_rows, kv_heads, HEAD_SIZE), k_gain), position
        )
        .astype(jnp.bfloat16)
        .reshape(local_rows, kv_heads * HEAD_SIZE)
    )
    values_flat = values_raw.astype(jnp.bfloat16)
    key_tags = jnp.where(key_mask == 1, segment_ids, -2).astype(jnp.bfloat16)
    row_segs = segment_ids.astype(jnp.float32)
    row_shared = shared_req.astype(jnp.float32)
    request_ids = jnp.arange(prompt_lengths.shape[0], dtype=jnp.int32)
    my_request = jnp.sum(jnp.where(cache_slot == device_seq, request_ids, 0))
    my_start = jnp.sum(jnp.where(request_ids == my_request, starts, 0))
    my_length = jnp.sum(jnp.where(request_ids == my_request, prompt_lengths, 0))
    offsets = jnp.arange(LMAX, dtype=jnp.int32)
    scale_factor = HEAD_SIZE ** (-0.5)

    def visible_of(tags_part, columns):
        own = tags_part[None, :] == row_segs[:, None]
        other = tags_part[None, :] == row_shared[:, None]
        earlier = columns[None, :] <= token_ids[:, None]
        diagonal = columns[None, :] == token_ids[:, None]
        return diagonal | earlier & (own | other)

    head_shape = (local_rows, kv_heads, query_group_width)
    soft_start = (
        jnp.full(head_shape, masked_score, jnp.float32),
        jnp.zeros(head_shape, jnp.float32),
        jnp.zeros(head_shape + (HEAD_SIZE,), jnp.float32),
    )
    empty_cache = jnp.zeros((LMAX, kv_heads * HEAD_SIZE), jnp.bfloat16)
    start_state = soft_start + (empty_cache, empty_cache)
    top_now, totals_now, summed_now, cache_k, cache_v = start_state
    piece_keys = lax.all_gather(flat_keys, "seq", axis=0, tiled=True)
    piece_values = lax.all_gather(values_flat, "seq", axis=0, tiled=True)
    piece_tags = lax.all_gather(key_tags, "seq", axis=0, tiled=True)
    piece_columns = jnp.arange(piece_keys.shape[0], dtype=jnp.int32)
    piece_rows = piece_keys.shape[0]
    block_keys = math.gcd(piece_rows, 1024)

    def key_block(block_index, loop_state):
        block_offset = block_index * block_keys
        keys_part = lax.dynamic_slice_in_dim(piece_keys, block_offset, block_keys, 0).reshape(
            block_keys, kv_heads, HEAD_SIZE
        )
        values_part = lax.dynamic_slice_in_dim(piece_values, block_offset, block_keys, 0).reshape(
            block_keys, kv_heads, HEAD_SIZE
        )
        tags_part = lax.dynamic_slice_in_dim(piece_tags, block_offset, block_keys, 0).astype(
            jnp.float32
        )
        columns = lax.dynamic_slice_in_dim(piece_columns, block_offset, block_keys, 0)
        visible = visible_of(tags_part, columns)
        old_top, old_totals, old_summed = loop_state
        allowed = visible[:, None, None, :]
        scores = (
            jnp.einsum("qhgd,khd->qhgk", query_rows, keys_part, preferred_element_type=jnp.float32)
            * scale_factor
        )
        scores = jnp.where(allowed, scores, masked_score)
        new_top = jnp.maximum(old_top, jnp.max(scores, axis=-1))
        factor = jnp.exp(old_top - new_top)
        raw_weights = jnp.where(allowed, jnp.exp(scores - new_top[..., None]), 0.0)
        new_totals = old_totals * factor + jnp.sum(raw_weights, axis=-1)
        new_summed = old_summed * factor[..., None] + jnp.einsum(
            "qhgk,khd->qhgd",
            raw_weights.astype(jnp.bfloat16),
            values_part,
            preferred_element_type=jnp.float32,
        )
        return (new_top, new_totals, new_summed)

    top_now, totals_now, summed_now = lax.fori_loop(
        0, piece_rows // block_keys, key_block, (top_now, totals_now, summed_now)
    )
    copy_cache_k = cache_k
    copy_cache_v = cache_v
    piece_rows = piece_keys.shape[0]
    wanted = my_start + offsets
    in_window = ((wanted >= 0) & (wanted < piece_rows) & (offsets < my_length))[:, None]
    source = jnp.clip(wanted, 0, piece_rows - 1)
    copy_cache_k = jnp.where(in_window, jnp.take(piece_keys, source, axis=0), copy_cache_k)
    copy_cache_v = jnp.where(in_window, jnp.take(piece_values, source, axis=0), copy_cache_v)
    cache_k = copy_cache_k
    cache_v = copy_cache_v
    top_score, totals, summed, cache_k, cache_v = (
        top_now,
        totals_now,
        summed_now,
        cache_k,
        cache_v,
    )
    attended = (summed / totals[..., None]).reshape(local_rows, query_heads * HEAD_SIZE)
    gated_heads = (attended * jax.nn.sigmoid(gate_logits)).astype(jnp.bfloat16)
    partial_out = jnp.dot(
        gated_heads,
        lax.all_gather(w_out, "seq", axis=1, tiled=True),
        preferred_element_type=jnp.float32,
    )
    branch_sum = lax.psum_scatter(
        partial_out.astype(jnp.bfloat16), "mdl", scatter_dimension=1, tiled=True
    ).astype(jnp.float32)
    layer_out = (wide_tokens + branch_sum).astype(jnp.bfloat16)
    return (layer_out, cache_k[None], cache_v[None])


def solution(mesh):
    placed = (
        P("seq", "mdl"),
        P("mdl"),
        P("seq", "mdl"),
        P("seq", "mdl"),
        P("seq", "mdl"),
        P("seq", "mdl"),
        P(),
        P(),
        P("mdl", "seq"),
        P(),
        P("seq"),
        P(),
        P("seq"),
        P(),
    )
    return jax.shard_map(
        body,
        mesh=mesh,
        in_specs=placed,
        out_specs=(P("seq", "mdl"), P("seq", None, "mdl"), P("seq", None, "mdl")),
        check_vma=False,
    )
```

profile of v0, /device:TPU:1, one launch (start us, length us, event | category | flops | bytes accessed | tf_op | source)
XLA Modules:
  0.0 971.2 jit_solution(3324895451097505820)
XLA Ops:
  8.3 8.3 psum.7
  28.4 16.6 %all-gather.10.cloned.1.call-done = bf16[256,2048]{1,0:T(8,128)(2,1)} async-done(((bf16[256,512]{1,0:T(8,128)(2,1)}), bf16[256,2048]{1,0:T(8,128)(2,1)}) %all-gather.10.cloned.1.call-update) | async-done | bytes 1048592 | tf_op jit(solution)/shard_map/all_gather | solution.py:72
  45.0 114.0 %all-gather.12.cloned.1.call-done = bf16[2048,256]{1,0:T(8,128)(2,1)} async-done(((bf16[32,256]{1,0:T(8,128)(2,1)}), bf16[2048,256]{1,0:T(8,128)(2,1)}) %all-gather.12.cloned.1.call-update) | async-done | bytes 1048592 | tf_op jit(solution)/shard_map/all_gather | solution.py:75
  162.2 111.6 %all-gather.18.cloned.1.call-done = bf16[2048,256]{1,0:T(8,128)(2,1)} async-done(((bf16[32,256]{1,0:T(8,128)(2,1)}), bf16[2048,256]{1,0:T(8,128)(2,1)}) %all-gather.18.cloned.1.call-update) | async-done | bytes 1048592 | tf_op jit(solution)/shard_map/all_gather | solution.py:76
  278.1 150.8 %all-gather = bf16[64,1,256]{2,1,0:T(2,128)(2,1)S(1)} all-gather(bf16[1,1,256]{2,1,0:T(2,128)(2,1)S(1)} %reshape.287), channel_id=1, replica_groups=mesh['seq'=64,'mdl'=4] {'seq'}, dimensions={0}, use_global_device_ids=true | all-gather | bytes 33280 | tf_op jit(solution)/shard_map/all_gather | solution.py:134
  433.1 113.0 %all-gather.14.cloned.1.call-done = bf16[16384,256]{1,0:T(8,128)(2,1)} async-done(((bf16[256,256]{1,0:T(8,128)(2,1)}), bf16[16384,256]{1,0:T(8,128)(2,1)}) %all-gather.14.cloned.1.call-update) | async-done | bytes 8388624 | tf_op jit(solution)/shard_map/all_gather | solution.py:132
  546.1 151.5 %all-gather.20.cloned.1.call-done = bf16[16384,256]{1,0:T(8,128)(2,1)} async-done(((bf16[256,256]{1,0:T(8,128)(2,1)}), bf16[16384,256]{1,0:T(8,128)(2,1)}) %all-gather.20.cloned.1.call-update) | async-done | bytes 8388624 | tf_op jit(solution)/shard_map/all_gather | solution.py:133
  697.6 202.7 %while.18 = (s32[]{:T(128)}, f32[256,2,2]{0,2,1:T(2,128)S(1)}, f32[256,2,2]{0,2,1:T(2,128)S(1)}, f32[256,2,2,128]{0,3,2,1:T(8,128)}, s32[16384]{0:T(1024)S(1)}, ...) while((s32[]{:T(128)}, f32[256,2,2]{0,2,1:T(2,128)S(1)}, ...), condition=%wide.region_11.12_spmd.clone, body=%wide.region_8.11_spmd.clone.sunk | while | flops 552737024 | bytes 24471832 | solution.py:171
  706.0 3.5 fusion.72
  718.6 3.5 fusion.72
  731.3 3.5 fusion.72
  744.0 3.5 fusion.72
  756.6 3.5 fusion.72
  765.8 3.2 fusion.70
  769.3 3.5 fusion.72
  782.0 3.5 fusion.72
  794.6 3.5 fusion.72
  803.8 3.2 fusion.70
  807.3 3.5 fusion.72
  820.0 3.5 fusion.72
  832.6 3.5 fusion.72
  845.3 3.5 fusion.72
  858.0 3.5 fusion.72
  870.6 3.5 fusion.72
  879.8 3.2 fusion.70
  883.3 3.5 fusion.72
  896.0 3.5 fusion.72
  901.6 33.2 %all-gather.24.cloned.1.call-done = bf16[512,2048]{0,1:T(8,128)(2,1)} async-done(((bf16[512,32]{0,1:T(8,128)(2,1)}), bf16[512,2048]{0,1:T(8,128)(2,1)}) %all-gather.24.cloned.1.call-update) | async-done | bytes 2097168 | tf_op jit(solution)/shard_map/all_gather | solution.py:195
  934.8 4.6 convolution_convert_fusion
  941.2 6.0 gather_fusion
  947.2 6.0 gather_fusion.1
  954.3 8.7 reduce-scatter.2.cloned.1.call-done
  (336 shorter events, 166.2 us)
Async XLA Ops:
  7.2 154.0 %copy-start.6 = (f32[128]{0:T(128)S(1)}, f32[128]{0:T(128)}, u32[]{:S(2)}) copy-start(f32[128]{0:T(128)} %param.25) | copy-start | bytes 1540
  7.2 270.8 %copy-start.4 = (s32[256]{0:T(256)S(1)}, s32[256]{0:T(256)}, u32[]{:S(2)}) copy-start(s32[256]{0:T(256)} %param.28) | copy-start | bytes 3076
  7.2 270.8 %copy-start.5 = (s32[256]{0:T(256)S(1)}, s32[256]{0:T(256)}, u32[]{:S(2)}) copy-start(s32[256]{0:T(256)} %param.30) | copy-start | bytes 3076
  7.2 37.8 %all-gather.10.cloned.1.call-start = ((), (), s32[]{:S(2)}) async-start(), calls=%async_computation.1 | async-start | bytes 1310720 | tf_op jit(solution)/shard_map/all_gather | solution.py:72
  19.1 140.0 %all-gather.12.cloned.1.call-start = ((), (), s32[]{:S(2)}) async-start(), calls=%async_computation.2 | async-start | bytes 1064960 | tf_op jit(solution)/shard_map/all_gather | solution.py:75
  19.8 253.9 %all-gather.18.cloned.1.call-start = ((), (), s32[]{:S(2)}) async-start(), calls=%async_computation.5 | async-start | bytes 1064960 | tf_op jit(solution)/shard_map/all_gather | solution.py:76
  20.6 408.5 %all-gather.16.cloned.1.call-start = ((), (), s32[]{:S(2)}) async-start(), calls=%async_computation.4 | async-start | bytes 2129920 | tf_op jit(solution)/shard_map/all_gather | solution.py:74
  21.1 525.0 %all-gather.14.cloned.1.call-start = ((), (), s32[]{:S(2)}) async-start(), calls=%async_computation.3 | async-start | bytes 8519680 | tf_op jit(solution)/shard_map/all_gather | solution.py:132
  45.0 384.1 %copy-start = (bf16[256,2048]{1,0:T(8,128)(2,1)S(1)}, bf16[256,2048]{1,0:T(8,128)(2,1)}, u32[]{:S(2)}) copy-start(bf16[256,2048]{1,0:T(8,128)(2,1)} %all-gather.10.cloned.1.call-done) | copy-start | bytes 3145732
  162.1 269.9 %copy-start.7 = (f32[128]{0:T(128)S(1)}, f32[128]{0:T(128)}, u32[]{:S(2)}) copy-start(f32[128]{0:T(128)} %param.24) | copy-start | bytes 1540
  162.1 535.5 %all-gather.20.cloned.1.call-start = ((), (), s32[]{:S(2)}) async-start(), calls=%async_computation.6 | async-start | bytes 8519680 | tf_op jit(solution)/shard_map/all_gather | solution.py:133
  276.4 625.2 %all-gather.22.cloned.1.call-start = ((), (), s32[]{:S(2)}) async-start(), calls=%async_computation.7 | async-start | bytes 2129920 | tf_op jit(solution)/shard_map/all_gather | solution.py:77
  277.2 657.7 %all-gather.24.cloned.1.call-start = ((), (), s32[]{:S(2)}) async-start(), calls=%async_computation.8 | async-start | bytes 2129920 | tf_op jit(solution)/shard_map/all_gather | solution.py:195
  277.9 685.1 %reduce-scatter.2.cloned.1.call-start = ((), (), s32[]{:S(2)}) async-start(), calls=%async_computation.9 | async-start | bytes 1310720 | tf_op jit(solution)/shard_map/reduce_scatter | solution.py:198
  699.7 6.3 copy-start.2
  709.5 0.9 copy-start.3
  712.3 6.3 copy-start.2
  725.0 6.3 copy-start.2
  737.6 6.3 copy-start.2
  750.3 6.3 copy-start.2
  763.0 6.3 copy-start.2
  775.6 6.3 copy-start.2
  788.3 6.3 copy-start.2
  801.0 6.3 copy-start.2
  813.6 6.3 copy-start.2
  826.3 6.3 copy-start.2
  839.0 6.3 copy-start.2
  851.6 6.3 copy-start.2
  864.3 6.3 copy-start.2
  876.9 6.3 copy-start.2
  889.6 6.3 copy-start.2
  939.4 23.5 %copy-start.1 = (bf16[256,512]{1,0:T(8,128)(2,1)S(1)}, bf16[256,512]{1,0:T(8,128)(2,1)}, u32[]{:S(2)}) copy-start(bf16[256,512]{1,0:T(8,128)(2,1)} %param.18) | copy-start | bytes 786436
  (15 other events, 12.8 us)
Sparse Core Ops, SparseCore 0:
  19.2 25.7 all-gather.9
  48.6 110.3 all-gather.11
  162.7 111.0 all-gather.17
  277.2 116.5 all-gather.15
  397.7 148.3 all-gather.13
  550.1 147.5 all-gather.19
  701.2 114.5 all-gather.21
  819.4 115.3 all-gather.23
  939.6 23.3 reduce-scatter.1
where the time goes:
time: 973 us; the launch traced here: 971 us
  waiting for transfers between devices  552 us (57%)
  blocking collectives  159 us (16%)
  matrix products  113 us (12%)
  other arithmetic  76.1 us (8%)
  local copies, waits for them, and re-layouts  55.5 us (6%)
  between operations  14.2 us (1%)
    all_gather x1, waiting for transfers between devices, body(): piece_values = lax.all_gather(values_flat, 'seq', axis=0, tiled=True)  152 us
    all_gather x1, blocking collectives, body(): piece_tags = lax.all_gather(key_tags, 'seq', axis=0, tiled=True)  151 us
    all_gather x1, waiting for transfers between devices, body(): lax.all_gather(key_matrix, 'seq', axis=0, tiled=True)  114 us
    all_gather x1, waiting for transfers between devices, body(): piece_keys = lax.all_gather(flat_keys, 'seq', axis=0, tiled=True)  113 us
    all_gather x1, waiting for transfers between devices, body(): lax.all_gather(value_matrix, 'seq', axis=0, tiled=True)  112 us
    dot_general x16, matrix products, key_block(): jnp.einsum('qhgk,khd->qhgd', raw_weights.astype(jnp.bfloat16), values_par...  55.6 us
    reduce_sum x16, other arithmetic, key_block(): new_totals = old_totals * factor + jnp.sum(raw_weights, axis=-1)  51.6 us
    dot_general x16, matrix products, key_block(): jnp.einsum('qhgd,khd->qhgk', query_rows, keys_part, preferred_element_typ...  45.6 us
  transfers between devices with their start and end apart: 9, of which 7 were waited for; matrix products, arithmetic and copies ran while one was open for 23% of the time, Pallas kernels for 0%

commit v1 on v0

--- a/solution.py
+++ b/solution.py
@@ -73,7 +73,9 @@
     pieces = (
         lax.all_gather(w_query, "seq", axis=0, tiled=True),
         lax.all_gather(key_matrix, "seq", axis=0, tiled=True),
-        lax.all_gather(value_matrix, "seq", axis=0, tiled=True),
+        jnp.concatenate(
+            lax.all_to_all(jnp.stack([value_matrix] * lax.axis_size("seq")), "seq", 0, 0), axis=0
+        ),
         lax.all_gather(w_gate, "seq", axis=0, tiled=True),
     )
     columns = normalized_input

time: 973 us -> 860 us (0.88)
  waiting for transfers between devices: 552 us -> 411 us
  blocking collectives: 159 us -> 188 us
    all_gather x1 -> x0, waiting for transfers between devices: 112 us -> none  [body(): lax.all_gather(value_matrix, 'seq', axis=0, tiled=True)]
    all_to_all x0 -> x1, blocking collectives: none -> 30.7 us  [body(): lax.all_to_all(jnp.stack([value_matrix] * lax.axis_size('seq')), 'seq', 0...]
    all_gather x1, waiting for transfers between devices: 113 us -> 84.4 us  [body(): piece_keys = lax.all_gather(flat_keys, 'seq', axis=0, tiled=True)]
  transfers between devices with their start and end apart: 9 -> 8, of which waited for: 7 -> 6; matrix products, arithmetic and copies ran while one was open for 23% -> 26% of each run, Pallas kernels for 0% -> 0%
where the time goes in v1:
time: 860 us; the launch traced here: 858 us
  waiting for transfers between devices  411 us (48%)
  blocking collectives  188 us (22%)
  matrix products  111 us (13%)
  other arithmetic  76.3 us (9%)
  local copies, waits for them, and re-layouts  55.4 us (6%)
  between operations  14.5 us (2%)
    all_gather x1, waiting for transfers between devices, body(): piece_values = lax.all_gather(values_flat, 'seq', axis=0, tiled=True)  152 us
    all_gather x1, blocking collectives, body(): piece_tags = lax.all_gather(key_tags, 'seq', axis=0, tiled=True)  149 us
    all_gather x1, waiting for transfers between devices, body(): lax.all_gather(key_matrix, 'seq', axis=0, tiled=True)  114 us
    all_gather x1, waiting for transfers between devices, body(): piece_keys = lax.all_gather(flat_keys, 'seq', axis=0, tiled=True)  84.4 us
    dot_general x16, matrix products, key_block(): jnp.einsum('qhgk,khd->qhgd', raw_weights.astype(jnp.bfloat16), values_par...  55.6 us
    reduce_sum x16, other arithmetic, key_block(): new_totals = old_totals * factor + jnp.sum(raw_weights, axis=-1)  51.6 us
    dot_general x16, matrix products, key_block(): jnp.einsum('qhgd,khd->qhgk', query_rows, keys_part, preferred_element_typ...  45.5 us
    all_gather x1, waiting for transfers between devices, body(): lax.all_gather(w_out, 'seq', axis=1, tiled=True)  33.3 us
  transfers between devices with their start and end apart: 8, of which 6 were waited for; matrix products, arithmetic and copies ran while one was open for 26% of the time, Pallas kernels for 0%

profile of v1, /device:TPU:1, one launch (start us, length us, event | category | flops | bytes accessed | tf_op | source)
XLA Modules:
  0.0 858.1 jit_solution(14100263104265946409)
XLA Ops:
  8.3 8.3 psum.7
  27.9 17.1 %all-gather.9.cloned.1.call-done = bf16[256,2048]{1,0:T(8,128)(2,1)} async-done(((bf16[256,512]{1,0:T(8,128)(2,1)}), bf16[256,2048]{1,0:T(8,128)(2,1)}) %all-gather.9.cloned.1.call-update) | async-done | bytes 1048592 | tf_op jit(solution)/shard_map/all_gather | solution.py:72
  45.0 114.0 %all-gather.11.cloned.1.call-done = bf16[2048,256]{1,0:T(8,128)(2,1)} async-done(((bf16[32,256]{1,0:T(8,128)(2,1)}), bf16[2048,256]{1,0:T(8,128)(2,1)}) %all-gather.11.cloned.1.call-update) | async-done | bytes 1048592 | tf_op jit(solution)/shard_map/all_gather | solution.py:75
  162.3 30.7 %all_to_all.5 = bf16[64,32,256]{2,1,0:T(8,128)(2,1)S(1)} all-to-all(bf16[64,32,256]{2,1,0:T(8,128)(2,1)S(1)} %stack.2), channel_id=1, replica_groups=mesh['seq'=64,'mdl'=4] {'seq'}, dimensions={0} | all-to-all | bytes 2097152 | tf_op jit(solution)/shard_map/all_to_all | solution.py:77
  195.6 148.8 %all-gather = bf16[64,1,256]{2,1,0:T(2,128)(2,1)S(1)} all-gather(bf16[1,1,256]{2,1,0:T(2,128)(2,1)S(1)} %reshape.293), channel_id=1, replica_groups=mesh['seq'=64,'mdl'=4] {'seq'}, dimensions={0}, use_global_device_ids=true | all-gather | bytes 33280 | tf_op jit(solution)/shard_map/all_gather | solution.py:136
  348.7 84.4 %all-gather.13.cloned.1.call-done = bf16[16384,256]{1,0:T(8,128)(2,1)} async-done(((bf16[256,256]{1,0:T(8,128)(2,1)}), bf16[16384,256]{1,0:T(8,128)(2,1)}) %all-gather.13.cloned.1.call-update) | async-done | bytes 8388624 | tf_op jit(solution)/shard_map/all_gather | solution.py:134
  433.1 151.5 %all-gather.17.cloned.1.call-done = bf16[16384,256]{1,0:T(8,128)(2,1)} async-done(((bf16[256,256]{1,0:T(8,128)(2,1)}), bf16[16384,256]{1,0:T(8,128)(2,1)}) %all-gather.17.cloned.1.call-update) | async-done | bytes 8388624 | tf_op jit(solution)/shard_map/all_gather | solution.py:135
  584.6 202.4 %while.18 = (s32[]{:T(128)}, f32[256,2,2]{0,2,1:T(2,128)S(1)}, f32[256,2,2]{0,2,1:T(2,128)S(1)}, f32[256,2,2,128]{0,3,2,1:T(8,128)}, s32[16384]{0:T(1024)S(1)}, ...) while((s32[]{:T(128)}, f32[256,2,2]{0,2,1:T(2,128)S(1)}, ...), condition=%wide.region_11.12_spmd.clone, body=%wide.region_8.11_spmd.clone.sunk | while | flops 552737024 | bytes 24471832 | solution.py:173
  592.9 3.5 fusion.72
  605.6 3.5 fusion.72
  618.2 3.5 fusion.72
  630.9 3.5 fusion.72
  643.5 3.5 fusion.72
  652.7 3.2 fusion.70
  656.1 3.5 fusion.72
  668.8 3.5 fusion.72
  681.4 3.5 fusion.72
  690.6 3.2 fusion.70
  694.1 3.5 fusion.72
  706.8 3.5 fusion.72
  719.4 3.5 fusion.72
  732.1 3.5 fusion.72
  744.7 3.5 fusion.72
  757.3 3.5 fusion.72
  766.5 3.2 fusion.70
  770.0 3.5 fusion.72
  782.6 3.5 fusion.72
  788.3 33.3 %all-gather.21.cloned.1.call-done = bf16[512,2048]{0,1:T(8,128)(2,1)} async-done(((bf16[512,32]{0,1:T(8,128)(2,1)}), bf16[512,2048]{0,1:T(8,128)(2,1)}) %all-gather.21.cloned.1.call-update) | async-done | bytes 2097168 | tf_op jit(solution)/shard_map/all_gather | solution.py:197
  821.6 4.6 convolution_convert_fusion
  828.2 6.0 gather_fusion
  834.3 6.0 gather_fusion.1
  841.3 8.3 reduce-scatter.2.cloned.1.call-done
  (337 shorter events, 164.0 us)
Async XLA Ops:
  7.2 154.0 %copy-start.7 = (f32[128]{0:T(128)S(1)}, f32[128]{0:T(128)}, u32[]{:S(2)}) copy-start(f32[128]{0:T(128)} %param.25) | copy-start | bytes 1540
  7.2 155.0 %copy-start.4 = (bf16[32,256]{1,0:T(8,128)(2,1)S(1)}, bf16[32,256]{1,0:T(8,128)(2,1)}, u32[]{:S(2)}) copy-start(bf16[32,256]{1,0:T(8,128)(2,1)} %param.22) | copy-start | bytes 49156
  7.2 37.8 %all-gather.9.cloned.1.call-start = ((), (), s32[]{:S(2)}) async-start(), calls=%async_computation.2 | async-start | bytes 1310720 | tf_op jit(solution)/shard_map/all_gather | solution.py:72
  19.1 140.0 %all-gather.11.cloned.1.call-start = ((), (), s32[]{:S(2)}) async-start(), calls=%async_computation.3 | async-start | bytes 1064960 | tf_op jit(solution)/shard_map/all_gather | solution.py:75
  19.8 324.8 %all-gather.15.cloned.1.call-start = ((), (), s32[]{:S(2)}) async-start(), calls=%async_computation.5 | async-start | bytes 2129920 | tf_op jit(solution)/shard_map/all_gather | solution.py:74
  20.6 412.5 %all-gather.13.cloned.1.call-start = ((), (), s32[]{:S(2)}) async-start(), calls=%async_computation.4 | async-start | bytes 8519680 | tf_op jit(solution)/shard_map/all_gather | solution.py:134
  45.0 148.0 %copy-start = (bf16[256,2048]{1,0:T(8,128)(2,1)S(1)}, bf16[256,2048]{1,0:T(8,128)(2,1)}, u32[]{:S(2)}) copy-start(bf16[256,2048]{1,0:T(8,128)(2,1)} %all-gather.9.cloned.1.call-done) | copy-start | bytes 3145732
  161.1 34.4 %copy-start.5 = (s32[256]{0:T(256)S(1)}, s32[256]{0:T(256)}, u32[]{:S(2)}) copy-start(s32[256]{0:T(256)} %param.28) | copy-start | bytes 3076
  161.2 34.4 %copy-start.6 = (s32[256]{0:T(256)S(1)}, s32[256]{0:T(256)}, u32[]{:S(2)}) copy-start(s32[256]{0:T(256)} %param.30) | copy-start | bytes 3076
  162.1 422.4 %all-gather.17.cloned.1.call-start = ((), (), s32[]{:S(2)}) async-start(), calls=%async_computation.6 | async-start | bytes 8519680 | tf_op jit(solution)/shard_map/all_gather | solution.py:135
  193.0 154.5 %copy-start.8 = (f32[128]{0:T(128)S(1)}, f32[128]{0:T(128)}, u32[]{:S(2)}) copy-start(f32[128]{0:T(128)} %param.24) | copy-start | bytes 1540
  194.2 594.1 %all-gather.19.cloned.1.call-start = ((), (), s32[]{:S(2)}) async-start(), calls=%async_computation.7 | async-start | bytes 2129920 | tf_op jit(solution)/shard_map/all_gather | solution.py:79
  194.7 626.9 %all-gather.21.cloned.1.call-start = ((), (), s32[]{:S(2)}) async-start(), calls=%async_computation.8 | async-start | bytes 2129920 | tf_op jit(solution)/shard_map/all_gather | solution.py:197
  195.5 654.1 %reduce-scatter.2.cloned.1.call-start = ((), (), s32[]{:S(2)}) async-start(), calls=%async_computation.9 | async-start | bytes 1310720 | tf_op jit(solution)/shard_map/reduce_scatter | solution.py:200
  586.6 6.3 copy-start.2
  596.4 0.8 copy-start.3
  599.2 6.3 copy-start.2
  611.9 6.3 copy-start.2
  624.5 6.3 copy-start.2
  637.2 6.3 copy-start.2
  649.8 6.3 copy-start.2
  662.5 6.3 copy-start.2
  675.1 6.3 copy-start.2
  687.8 6.3 copy-start.2
  700.4 6.3 copy-start.2
  713.1 6.3 copy-start.2
  725.7 6.3 copy-start.2
  738.4 6.3 copy-start.2
  751.0 6.3 copy-start.2
  763.6 6.3 copy-start.2
  776.3 6.3 copy-start.2
  826.2 23.4 %copy-start.1 = (bf16[256,512]{1,0:T(8,128)(2,1)S(1)}, bf16[256,512]{1,0:T(8,128)(2,1)}, u32[]{:S(2)}) copy-start(bf16[256,512]{1,0:T(8,128)(2,1)} %param.18) | copy-start | bytes 786436
  (15 other events, 12.7 us)
Sparse Core Ops, SparseCore 0:
  19.2 25.7 all-gather.8
  48.6 110.3 all-gather.10
  162.7 117.9 all-gather.14
  284.6 148.4 all-gather.12
  437.0 147.5 all-gather.16
  588.0 114.5 all-gather.18
  706.2 115.3 all-gather.20
  826.4 23.1 reduce-scatter.1
